TPU v7x, 32 devices: a whole 2x2x4 slice. The times are simulated.
32 devices in a mesh: pts: 4 (over x, core), snap: 8 (over z, y).
Axes of the slice: x: 2, y: 2, z: 4, core: 2. Of those that a mesh axis runs over, the one named last changes fastest.
Arguments:
- snapshots: float32 [4096, 8192], P('pts', 'snap'), may hold values from -8 to 8
- modes_init: float32 [4096, 128], P('pts'), may hold values from -6 to 6
- coefs_init: float32 [128, 8192], P(None, 'snap'), may hold values from -0.09375 to 0.09375
Outputs:
- modes: float32 [4096, 128], P('pts')
- amplitudes: float32 [128, 8192], P(None, 'snap')
All inputs are finite; a program needn't handle non-finite values.
Results may differ from a plain program's by a relative error of at most 0.0003.
Values sent between devices are 32-bit elements; how exact they have to be, the bound alone decides.
A program may use at most 64 MiB of HBM per device.

v0:
```python
import jax
import jax.numpy as jnp
from jax import lax
from jax.sharding import PartitionSpec as P

OUTER = 2
INNER = 2
HUBER = 1.345
RIDGE = 0.01


def high_dot(left, right):
    return jnp.dot(left, right, preferred_element_type=jnp.float32, precision=lax.Precision.HIGHEST)


def clipped_error(snapshots, modes, coefs, count):
    error = snapshots - high_dot(modes, coefs)
    total = lax.psum(jnp.sum(error * error), ("pts", "snap"))
    limit = HUBER * jnp.sqrt(total / count + 1e-06)
    return jnp.clip(error, -limit, limit)


def shards(snapshots, modes_init, coefs_init):
    modes = modes_init
    coefs = coefs_init
    rows, width = snapshots.shape
    points = rows * lax.axis_size("pts")
    count = float(points * width * lax.axis_size("snap"))
    rank = modes.shape[1]
    eye = jnp.eye(rank, dtype=jnp.float32)
    for outer in range(OUTER):
        gram = lax.psum(high_dot(modes.T, modes), "pts") + RIDGE * eye
        factor = jnp.linalg.cholesky(gram)
        for inner in range(INNER):
            clipped = clipped_error(snapshots, modes, coefs, count)
            product = high_dot(modes.T, clipped)
            share = lax.psum_scatter(product, "pts", scatter_dimension=1, tiled=True)
            span = share.shape[1]
            own = lax.dynamic_slice_in_dim(coefs, lax.axis_index("pts") * span, span, 1)
            own = own + jax.scipy.linalg.cho_solve((factor, True), share)
            coefs = lax.all_gather(own, "pts", axis=1, tiled=True)
        clipped = clipped_error(snapshots, modes, coefs, count)
        hess = lax.psum(high_dot(coefs, coefs.T), "snap") + RIDGE * eye
        hfactor = jnp.linalg.cholesky(hess)
        moment = high_dot(clipped, coefs.T)
        summed = lax.psum(moment, "snap")
        modes = modes + jax.scipy.linalg.cho_solve((hfactor, True), summed.T).T
    return (modes, coefs * jnp.sqrt(jnp.float32(points)))


def solution(mesh):
    in_specs = (P("pts", "snap"), P("pts", None), P(None, "snap"))
    out_specs = (P("pts", None), P(None, "snap"))
    return jax.shard_map(shards, mesh=mesh, in_specs=in_specs, out_specs=out_specs, check_vma=False)
```

profile of v0, /device:TPU:0, one launch (start us, length us, event | category | flops | bytes accessed | tf_op | source)
XLA Modules:
  0.0 692.1 jit_solution(7492501816023668363)
XLA Ops:
  10.1 8.6 %multiply_reduce_fusion.5 = (f32[]{:T(128)}, f32[1024,1024]{1,0:T(8,128)}) fusion(f32[1024,1024]{1,0:T(8,128)} %param.8, f32[1024,128]{1,0:T(8,128)} %param.9, f32[128,1024]{1,0:T(8,128)} %param.10), kind=kOutput, calls=%fused_computation.25 | convolution fusion | flops 1613758464 | bytes 9437188 | tf_op jit(solution)/shard_map/dot_general | solution.py:13
  18.8 42.5 %psum.85 = f32[]{:T(128)} all-reduce(f32[]{:T(128)} %get-tuple-element.11), channel_id=1, replica_groups=mesh['pts'=4,'snap'=8] {'pts','snap'}, use_global_device_ids=true, to_apply=%region_4.6 | all-reduce | flops 1 | bytes 8 | tf_op jit(solution)/shard_map/psum | solution.py:18
  61.9 9.6 %fusion.32 = f32[128,1024]{0,1:T(8,128)} fusion(f32[1024,128]{1,0:T(8,128)S(1)} %copy-done, f32[1024,1024]{1,0:T(8,128)} %get-tuple-element.12, f32[]{:T(128)S(6)} %neg.18, f32[]{:T(128)S(6)} %mul.63), kind=kOutput, calls=%fused_computation.46 | convolution fusion | flops 1612709888 | bytes 5242888 | tf_op jit(solution)/shard_map/dot_general | solution.py:13
  79.4 11.7 %cholesky.74 = f32[128,128]{1,0:T(8,128)S(1)} custom-call(f32[128,128]{1,0:T(8,128)S(1)} %fusion.63), custom_call_target="Cholesky" | custom-call | tf_op jit(solution)/shard_map/jit(cholesky)/cholesky | solution.py:33
  92.4 9.8 %custom-call.16 = f32[1,128,128]{1,2,0:T(8,128)S(1)} custom-call(f32[1,128,128]{2,1,0:T(8,128)S(1)} %fusion.38), custom_call_target="InvertDiagBlocksLowerTriangular" | custom-call | tf_op jit(solution)/shard_map/jit(_cho_solve)/triangular_solve | solution.py:40
  104.7 8.0 %all_gather.12 = f32[128,1024]{1,0:T(8,128)S(1)} all-gather(f32[128,256]{1,0:T(8,128)S(1)} %convolution_add_fusion.3), channel_id=1, replica_groups=mesh['pts'=4,'snap'=8] {'pts'}, dimensions={1}, use_global_device_ids=true | all-gather | bytes 655360 | tf_op jit(solution)/shard_map/all_gather | solution.py:41
  112.6 7.7 %multiply_reduce_fusion.4 = (f32[]{:T(128)}, f32[1024,1024]{0,1:T(8,128)}) fusion(f32[1024,1024]{0,1:T(8,128)} %copy.7, f32[128,1024]{1,0:T(8,128)S(1)} %all_gather.12, f32[1024,128]{1,0:T(8,128)S(1)} %copy-done), kind=kOutput, calls=%fused_computation.21 | convolution fusion | flops 1613758464 | bytes 9437188 | tf_op jit(solution)/shard_map/dot_general | solution.py:13
  120.3 39.7 %psum.86 = f32[]{:T(128)} all-reduce(f32[]{:T(128)} %get-tuple-element.13), channel_id=1, replica_groups=mesh['pts'=4,'snap'=8] {'pts','snap'}, use_global_device_ids=true, to_apply=%region_7.10 | all-reduce | flops 1 | bytes 8 | tf_op jit(solution)/shard_map/psum | solution.py:18
  167.2 22.0 %reduce-scatter.7.cloned.1.call-done = f32[128,256]{0,1:T(8,128)} async-done(((f32[128,1024]{0,1:T(8,128)}), f32[128,256]{0,1:T(8,128)}) %reduce-scatter.7.cloned.1.call-update) | async-done | bytes 131088 | tf_op jit(solution)/shard_map/reduce_scatter | solution.py:37
  197.3 7.6 %multiply_reduce_fusion.3 = (f32[]{:T(128)}, f32[1024,1024]{0,1:T(8,128)}) fusion(f32[1024,1024]{0,1:T(8,128)} %copy.7, f32[128,1024]{1,0:T(8,128)S(1)} %all_gather.13, f32[1024,128]{1,0:T(8,128)S(1)} %copy-done), kind=kOutput, calls=%fused_computation.17 | convolution fusion | flops 1613758464 | bytes 9437188 | tf_op jit(solution)/shard_map/dot_general | solution.py:13
  206.1 40.0 %psum.88 = f32[]{:T(128)} all-reduce(f32[]{:T(128)} %get-tuple-element.15), channel_id=1, replica_groups=mesh['pts'=4,'snap'=8] {'pts','snap'}, use_global_device_ids=true, to_apply=%region_11.14 | all-reduce | flops 1 | bytes 8 | tf_op jit(solution)/shard_map/psum | solution.py:18
  253.0 73.4 %all-reduce.13.cloned.1.call-done = (f32[128,1024]{1,0:T(8,128)}, f32[128,128]{0,1:T(8,128)}) async-done(((f32[128,1024]{1,0:T(8,128)}, f32[128,128]{0,1:T(8,128)}), (f32[128,1024]{1,0:T(8,128)}, f32[128,128]{0,1:T(8,128)})) %all-reduce.13.cloned.1.call-update) | async-done | bytes 589840 | tf_op jit(solution)/shard_map/psum | solution.py:46
  328.2 11.7 %cholesky.85 = f32[128,128]{1,0:T(8,128)S(1)} custom-call(f32[128,128]{1,0:T(8,128)S(1)} %fusion.56), custom_call_target="Cholesky" | custom-call | tf_op jit(solution)/shard_map/jit(cholesky)/cholesky | solution.py:44
  341.3 9.8 %custom-call.18 = f32[1,128,128]{1,2,0:T(8,128)S(1)} custom-call(f32[1,128,128]{2,1,0:T(8,128)S(1)} %fusion.39), custom_call_target="InvertDiagBlocksLowerTriangular" | custom-call | tf_op jit(solution)/shard_map/jit(_cho_solve)/triangular_solve | solution.py:47
  362.2 40.0 %psum.91 = f32[]{:T(128)} all-reduce(f32[]{:T(128)} %get-tuple-element.17), channel_id=1, replica_groups=mesh['pts'=4,'snap'=8] {'pts','snap'}, use_global_device_ids=true, to_apply=%region_15.19 | all-reduce | flops 1 | bytes 8 | tf_op jit(solution)/shard_map/psum | solution.py:18
  410.5 11.7 %cholesky.96 = f32[128,128]{1,0:T(8,128)S(1)} custom-call(f32[128,128]{1,0:T(8,128)S(1)} %fusion.52), custom_call_target="Cholesky" | custom-call | tf_op jit(solution)/shard_map/jit(cholesky)/cholesky | solution.py:33
  423.6 9.8 %custom-call.19 = f32[1,128,128]{1,2,0:T(8,128)S(1)} custom-call(f32[1,128,128]{2,1,0:T(8,128)S(1)} %fusion.40), custom_call_target="InvertDiagBlocksLowerTriangular" | custom-call | tf_op jit(solution)/shard_map/jit(_cho_solve)/triangular_solve | solution.py:40
  434.9 8.1 %all_gather.14 = f32[128,1024]{1,0:T(8,128)S(1)} all-gather(f32[128,256]{1,0:T(8,128)S(1)} %convolution_add_fusion.1), channel_id=1, replica_groups=mesh['pts'=4,'snap'=8] {'pts'}, dimensions={1}, use_global_device_ids=true | all-gather | bytes 655360 | tf_op jit(solution)/shard_map/all_gather | solution.py:41
  450.6 38.7 %psum.92 = f32[]{:T(128)} all-reduce(f32[]{:T(128)} %get-tuple-element.19), channel_id=1, replica_groups=mesh['pts'=4,'snap'=8] {'pts','snap'}, use_global_device_ids=true, to_apply=%region_18.22 | all-reduce | flops 1 | bytes 8 | tf_op jit(solution)/shard_map/psum | solution.py:18
  495.8 22.3 %reduce-scatter.11.cloned.1.call-done = f32[128,256]{1,0:T(8,128)} async-done(((f32[128,1024]{1,0:T(8,128)}), f32[128,256]{1,0:T(8,128)}) %reduce-scatter.11.cloned.1.call-update) | async-done | bytes 131088 | tf_op jit(solution)/shard_map/reduce_scatter | solution.py:37
  535.0 40.2 %psum.94 = f32[]{:T(128)} all-reduce(f32[]{:T(128)} %get-tuple-element.21), channel_id=1, replica_groups=mesh['pts'=4,'snap'=8] {'pts','snap'}, use_global_device_ids=true, to_apply=%region_22.26 | all-reduce | flops 1 | bytes 8 | tf_op jit(solution)/shard_map/psum | solution.py:18
  584.1 73.0 %all-reduce.11.cloned.1.call-done = (f32[128,1024]{1,0:T(8,128)}, f32[128,128]{0,1:T(8,128)}) async-done(((f32[128,1024]{1,0:T(8,128)}, f32[128,128]{0,1:T(8,128)}), (f32[128,1024]{1,0:T(8,128)}, f32[128,128]{0,1:T(8,128)})) %all-reduce.11.cloned.1.call-update) | async-done | bytes 589840 | tf_op jit(solution)/shard_map/psum | solution.py:46
  658.9 11.7 %cholesky.107 = f32[128,128]{1,0:T(8,128)S(1)} custom-call(f32[128,128]{1,0:T(8,128)S(1)} %fusion.45), custom_call_target="Cholesky" | custom-call | tf_op jit(solution)/shard_map/jit(cholesky)/cholesky | solution.py:44
  672.0 9.8 %custom-call.21 = f32[1,128,128]{1,2,0:T(8,128)S(1)} custom-call(f32[1,128,128]{2,1,0:T(8,128)S(1)} %fusion.41), custom_call_target="InvertDiagBlocksLowerTriangular" | custom-call | tf_op jit(solution)/shard_map/jit(_cho_solve)/triangular_solve | solution.py:47
  (76 shorter events, 105.7 us)
Async XLA Ops:
  7.2 70.4 %all-reduce.7.cloned.1.call-start = ((), (), s32[]{:S(2)}) async-start(), calls=%async_computation.4 | async-start | bytes 131072 | tf_op jit(solution)/shard_map/psum | solution.py:32
  10.1 51.9 %copy-start = (f32[1024,128]{1,0:T(8,128)S(1)}, f32[1024,128]{1,0:T(8,128)}, u32[]{:S(2)}) copy-start(f32[1024,128]{1,0:T(8,128)} %param.9) | copy-start | bytes 1572868
  10.1 92.2 %reduce-scatter.5.cloned.1.call-start = ((), (), s32[]{:S(2)}) async-start(), calls=%async_computation.5 | async-start | bytes 655360 | tf_op jit(solution)/shard_map/reduce_scatter | solution.py:37
  71.6 117.6 %reduce-scatter.7.cloned.1.call-start = ((), (), s32[]{:S(2)}) async-start(), calls=%async_computation.6 | async-start | bytes 655360 | tf_op jit(solution)/shard_map/reduce_scatter | solution.py:37
  167.1 159.3 %all-reduce.13.cloned.1.call-start = ((), (), s32[]{:S(2)}) async-start(), calls=%async_computation.11 | async-start | bytes 1179648 | tf_op jit(solution)/shard_map/psum | solution.py:46
  252.5 156.2 %all-reduce.9.cloned.1.call-start = ((), (), s32[]{:S(2)}) async-start(), calls=%async_computation.7 | async-start | bytes 131072 | tf_op jit(solution)/shard_map/psum | solution.py:32
  362.2 71.2 %reduce-scatter.9.cloned.1.call-start = ((), (), s32[]{:S(2)}) async-start(), calls=%async_computation.8 | async-start | bytes 655360 | tf_op jit(solution)/shard_map/reduce_scatter | solution.py:37
  408.6 109.5 %reduce-scatter.11.cloned.1.call-start = ((), (), s32[]{:S(2)}) async-start(), calls=%async_computation.9 | async-start | bytes 655360 | tf_op jit(solution)/shard_map/reduce_scatter | solution.py:37
  495.8 161.4 %all-reduce.11.cloned.1.call-start = ((), (), s32[]{:S(2)}) async-start(), calls=%async_computation.10 | async-start | bytes 1179648 | tf_op jit(solution)/shard_map/psum | solution.py:46
Sparse Core Ops, SparseCore 0:
  10.9 34.2 all-reduce.6
  71.7 21.8 reduce-scatter.4
  167.3 21.8 reduce-scatter.6
  252.7 73.7 all-reduce.12
  362.3 30.6 all-reduce.8
  408.8 21.6 reduce-scatter.8
  495.9 22.2 reduce-scatter.10
  583.4 73.6 all-reduce.10
where the time goes:
time: 698 us; the launch traced here: 692 us
  blocking collectives  270 us (39%)
  waiting for transfers between devices  191 us (27%)
  matrix products  105 us (15%)
  other arithmetic  99.1 us (14%)
  between operations  18.8 us (3%)
    psum x6, blocking collectives, clipped_error(): total = lax.psum(jnp.sum(error * error), ('pts', 'snap'))  241 us
    psum x2, waiting for transfers between devices, shards(): summed = lax.psum(moment, 'snap')  146 us
    dot_general x16, matrix products, high_dot(): jnp.dot(left, right, preferred_element_type=jnp.float32, precision=lax.Pr...  93.5 us
    reduce_scatter x4, waiting for transfers between devices, shards(): share = lax.psum_scatter(product, 'pts', scatter_dimension=1, tiled=True)  44.4 us
    all_gather x4, blocking collectives, shards(): coefs = lax.all_gather(own, 'pts', axis=1, tiled=True)  29.3 us
    another operation x6, other arithmetic, shards(): factor = jnp.linalg.cholesky(gram)  24.8 us
    another operation x6, other arithmetic, shards(): hfactor = jnp.linalg.cholesky(hess)  24.8 us
    another operation x4, other arithmetic, shards(): own = own + jax.scipy.linalg.cho_solve((factor, True), share)  20.9 us
  transfers between devices with their start and end apart: 8, of which 4 were waited for; matrix products, arithmetic and copies ran while one was open for 12% of the time, Pallas kernels for 0%

commit v1 on v0

--- a/solution.py
+++ b/solution.py
@@ -43,7 +43,7 @@
         hess = lax.psum(high_dot(coefs, coefs.T), "snap") + RIDGE * eye
         hfactor = jnp.linalg.cholesky(hess)
         moment = high_dot(clipped, coefs.T)
-        summed = lax.psum(moment, "snap")
+        summed = jnp.sum(lax.all_gather(moment, "snap"), axis=0)
         modes = modes + jax.scipy.linalg.cho_solve((hfactor, True), summed.T).T
     return (modes, coefs * jnp.sqrt(jnp.float32(points)))
 

time: 698 us -> 699 us (level)
    psum x2, waiting for transfers between devices: 146 us -> 40.1 us  [shards(): hess = lax.psum(high_dot(coefs, coefs.T), 'snap') + RIDGE * eye]
    all_gather x0 -> x2, waiting for transfers between devices: none -> 101 us  [shards(): summed = jnp.sum(lax.all_gather(moment, 'snap'), axis=0)]
  transfers between devices with their start and end apart: 8 -> 10, of which waited for: 4 -> 6; matrix products, arithmetic and copies ran while one was open for 12% -> 21% of each run, Pallas kernels for 0% -> 0%
where the time goes in v1:
time: 699 us; the launch traced here: 694 us
  blocking collectives  271 us (39%)
  waiting for transfers between devices  186 us (27%)
  matrix products  106 us (15%)
  other arithmetic  104 us (15%)
  between operations  19.1 us (3%)
    psum x6, blocking collectives, clipped_error(): total = lax.psum(jnp.sum(error * error), ('pts', 'snap'))  242 us
    all_gather x2, waiting for transfers between devices, shards(): summed = jnp.sum(lax.all_gather(moment, 'snap'), axis=0)  101 us
    dot_general x16, matrix products, high_dot(): jnp.dot(left, right, preferred_element_type=jnp.float32, precision=lax.Pr...  96.6 us
    reduce_scatter x4, waiting for transfers between devices, shards(): share = lax.psum_scatter(product, 'pts', scatter_dimension=1, tiled=True)  44 us
    psum x2, waiting for transfers between devices, shards(): hess = lax.psum(high_dot(coefs, coefs.T), 'snap') + RIDGE * eye  40.1 us
    all_gather x4, blocking collectives, shards(): coefs = lax.all_gather(own, 'pts', axis=1, tiled=True)  29.3 us
    another operation x6, other arithmetic, shards(): hfactor = jnp.linalg.cholesky(hess)  24.8 us
    another operation x6, other arithmetic, shards(): factor = jnp.linalg.cholesky(gram)  24.8 us
  transfers between devices with their start and end apart: 10, of which 6 were waited for; matrix products, arithmetic and copies ran while one was open for 21% of the time, Pallas kernels for 0%

profile of v1, /device:TPU:0, one launch (start us, length us, event | category | flops | bytes accessed | tf_op | source)
XLA Modules:
  0.0 693.6 jit_solution(12822842193598607610)
XLA Ops:
  10.1 8.6 %multiply_reduce_fusion.5 = (f32[]{:T(128)}, f32[1024,1024]{1,0:T(8,128)}) fusion(f32[1024,1024]{1,0:T(8,128)} %param.8, f32[1024,128]{1,0:T(8,128)} %param.9, f32[128,1024]{1,0:T(8,128)} %param.10), kind=kOutput, calls=%fused_computation.25 | convolution fusion | flops 1613758464 | bytes 9437188 | tf_op jit(solution)/shard_map/dot_general | solution.py:13
  18.8 42.7 %psum.71 = f32[]{:T(128)} all-reduce(f32[]{:T(128)} %get-tuple-element.7), channel_id=1, replica_groups=mesh['pts'=4,'snap'=8] {'pts','snap'}, use_global_device_ids=true, to_apply=%region_4.6 | all-reduce | flops 1 | bytes 8 | tf_op jit(solution)/shard_map/psum | solution.py:18
  62.2 9.6 %fusion.32 = f32[128,1024]{0,1:T(8,128)} fusion(f32[1024,128]{1,0:T(8,128)S(1)} %copy-done, f32[1024,1024]{1,0:T(8,128)} %get-tuple-element.8, f32[]{:T(128)S(6)} %neg.18, f32[]{:T(128)S(6)} %mul.63), kind=kOutput, calls=%fused_computation.46 | convolution fusion | flops 1612709888 | bytes 5242888 | tf_op jit(solution)/shard_map/dot_general | solution.py:13
  79.2 11.7 %cholesky.74 = f32[128,128]{1,0:T(8,128)S(1)} custom-call(f32[128,128]{1,0:T(8,128)S(1)} %fusion.65), custom_call_target="Cholesky" | custom-call | tf_op jit(solution)/shard_map/jit(cholesky)/cholesky | solution.py:33
  92.3 9.8 %custom-call.16 = f32[1,128,128]{1,2,0:T(8,128)S(1)} custom-call(f32[1,128,128]{2,1,0:T(8,128)S(1)} %fusion.42), custom_call_target="InvertDiagBlocksLowerTriangular" | custom-call | tf_op jit(solution)/shard_map/jit(_cho_solve)/triangular_solve | solution.py:40
  120.2 39.8 %psum.72 = f32[]{:T(128)} all-reduce(f32[]{:T(128)} %get-tuple-element.9), channel_id=1, replica_groups=mesh['pts'=4,'snap'=8] {'pts','snap'}, use_global_device_ids=true, to_apply=%region_7.10 | all-reduce | flops 1 | bytes 8 | tf_op jit(solution)/shard_map/psum | solution.py:18
  167.1 22.0 %reduce-scatter.7.cloned.1.call-done = f32[128,256]{0,1:T(8,128)} async-done(((f32[128,1024]{0,1:T(8,128)}), f32[128,256]{0,1:T(8,128)}) %reduce-scatter.7.cloned.1.call-update) | async-done | bytes 131088 | tf_op jit(solution)/shard_map/reduce_scatter | solution.py:37
  206.1 40.4 %psum.74 = f32[]{:T(128)} all-reduce(f32[]{:T(128)} %get-tuple-element.11), channel_id=1, replica_groups=mesh['pts'=4,'snap'=8] {'pts','snap'}, use_global_device_ids=true, to_apply=%region_11.14 | all-reduce | flops 1 | bytes 8 | tf_op jit(solution)/shard_map/psum | solution.py:18
  247.2 9.6 %fusion.9 = f32[1024,128]{1,0:T(8,128)} fusion(f32[128,1024]{1,0:T(8,128)S(1)} %all_gather.25, f32[1024,1024]{0,1:T(8,128)} %get-tuple-element.12, f32[]{:T(128)S(6)} %neg.20, f32[]{:T(128)S(6)} %mul.67), kind=kOutput, calls=%fused_computation.14 | convolution fusion | flops 1612709888 | bytes 5242888 | tf_op jit(solution)/shard_map/dot_general | solution.py:13
  257.6 18.5 %all-reduce.7.cloned.1.call-done = f32[128,128]{0,1:T(8,128)} async-done(((f32[128,128]{0,1:T(8,128)}), f32[128,128]{0,1:T(8,128)}) %all-reduce.7.cloned.1.call-update) | async-done | bytes 65552 | tf_op jit(solution)/shard_map/psum | solution.py:43
  277.9 11.7 %cholesky.85 = f32[128,128]{1,0:T(8,128)S(1)} custom-call(f32[128,128]{1,0:T(8,128)S(1)} %fusion.58), custom_call_target="Cholesky" | custom-call | tf_op jit(solution)/shard_map/jit(cholesky)/cholesky | solution.py:44
  290.9 9.8 %custom-call.18 = f32[1,128,128]{1,2,0:T(8,128)S(1)} custom-call(f32[1,128,128]{2,1,0:T(8,128)S(1)} %fusion.43), custom_call_target="InvertDiagBlocksLowerTriangular" | custom-call | tf_op jit(solution)/shard_map/jit(_cho_solve)/triangular_solve | solution.py:47
  300.7 50.7 %all-gather.5.cloned.1.call-done = f32[8192,128]{1,0:T(8,128)} async-done(((f32[1024,128]{1,0:T(8,128)}), f32[8192,128]{1,0:T(8,128)}) %all-gather.5.cloned.1.call-update) | async-done | bytes 4194320 | tf_op jit(solution)/shard_map/all_gather | solution.py:46
  364.0 39.3 %psum.76 = f32[]{:T(128)} all-reduce(f32[]{:T(128)} %get-tuple-element.13), channel_id=1, replica_groups=mesh['pts'=4,'snap'=8] {'pts','snap'}, use_global_device_ids=true, to_apply=%region_15.19 | all-reduce | flops 1 | bytes 8 | tf_op jit(solution)/shard_map/psum | solution.py:18
  411.6 11.7 %cholesky.96 = f32[128,128]{1,0:T(8,128)S(1)} custom-call(f32[128,128]{1,0:T(8,128)S(1)} %fusion.55), custom_call_target="Cholesky" | custom-call | tf_op jit(solution)/shard_map/jit(cholesky)/cholesky | solution.py:33
  424.7 9.8 %custom-call.19 = f32[1,128,128]{1,2,0:T(8,128)S(1)} custom-call(f32[1,128,128]{2,1,0:T(8,128)S(1)} %fusion.44), custom_call_target="InvertDiagBlocksLowerTriangular" | custom-call | tf_op jit(solution)/shard_map/jit(_cho_solve)/triangular_solve | solution.py:40
  436.0 8.2 %all_gather.28 = f32[128,1024]{1,0:T(8,128)S(1)} all-gather(f32[128,256]{1,0:T(8,128)S(1)} %convolution_add_fusion.1), channel_id=1, replica_groups=mesh['pts'=4,'snap'=8] {'pts'}, dimensions={1}, use_global_device_ids=true | all-gather | bytes 655360 | tf_op jit(solution)/shard_map/all_gather | solution.py:41
  451.7 39.1 %psum.77 = f32[]{:T(128)} all-reduce(f32[]{:T(128)} %get-tuple-element.15), channel_id=1, replica_groups=mesh['pts'=4,'snap'=8] {'pts','snap'}, use_global_device_ids=true, to_apply=%region_18.22 | all-reduce | flops 1 | bytes 8 | tf_op jit(solution)/shard_map/psum | solution.py:18
  497.3 22.0 %reduce-scatter.11.cloned.1.call-done = f32[128,256]{1,0:T(8,128)} async-done(((f32[128,1024]{1,0:T(8,128)}), f32[128,256]{1,0:T(8,128)}) %reduce-scatter.11.cloned.1.call-update) | async-done | bytes 131088 | tf_op jit(solution)/shard_map/reduce_scatter | solution.py:37
  536.3 40.4 %psum.79 = f32[]{:T(128)} all-reduce(f32[]{:T(128)} %get-tuple-element.17), channel_id=1, replica_groups=mesh['pts'=4,'snap'=8] {'pts','snap'}, use_global_device_ids=true, to_apply=%region_22.26 | all-reduce | flops 1 | bytes 8 | tf_op jit(solution)/shard_map/psum | solution.py:18
  584.6 21.7 %all-reduce.11.cloned.1.call-done = f32[128,128]{0,1:T(8,128)} async-done(((f32[128,128]{0,1:T(8,128)}), f32[128,128]{0,1:T(8,128)}) %all-reduce.11.cloned.1.call-update) | async-done | bytes 65552 | tf_op jit(solution)/shard_map/psum | solution.py:43
  608.0 11.7 %cholesky.107 = f32[128,128]{1,0:T(8,128)S(1)} custom-call(f32[128,128]{1,0:T(8,128)S(1)} %fusion.48), custom_call_target="Cholesky" | custom-call | tf_op jit(solution)/shard_map/jit(cholesky)/cholesky | solution.py:44
  621.1 9.8 %custom-call.21 = f32[1,128,128]{1,2,0:T(8,128)S(1)} custom-call(f32[1,128,128]{2,1,0:T(8,128)S(1)} %fusion.45), custom_call_target="InvertDiagBlocksLowerTriangular" | custom-call | tf_op jit(solution)/shard_map/jit(_cho_solve)/triangular_solve | solution.py:47
  630.9 50.7 %all-gather.7.cloned.1.call-done = f32[8192,128]{1,0:T(8,128)} async-done(((f32[1024,128]{1,0:T(8,128)}), f32[8192,128]{1,0:T(8,128)}) %all-gather.7.cloned.1.call-update) | async-done | bytes 4194320 | tf_op jit(solution)/shard_map/all_gather | solution.py:46
  (84 shorter events, 125.2 us)
Async XLA Ops:
  7.2 70.2 %all-reduce.5.cloned.1.call-start = ((), (), s32[]{:S(2)}) async-start(), calls=%async_computation.4 | async-start | bytes 131072 | tf_op jit(solution)/shard_map/psum | solution.py:32
  10.1 52.1 %copy-start = (f32[1024,128]{1,0:T(8,128)S(1)}, f32[1024,128]{1,0:T(8,128)}, u32[]{:S(2)}) copy-start(f32[1024,128]{1,0:T(8,128)} %param.9) | copy-start | bytes 1572868
  10.1 92.0 %reduce-scatter.5.cloned.1.call-start = ((), (), s32[]{:S(2)}) async-start(), calls=%async_computation.5 | async-start | bytes 655360 | tf_op jit(solution)/shard_map/reduce_scatter | solution.py:37
  71.8 117.3 %reduce-scatter.7.cloned.1.call-start = ((), (), s32[]{:S(2)}) async-start(), calls=%async_computation.6 | async-start | bytes 655360 | tf_op jit(solution)/shard_map/reduce_scatter | solution.py:37
  167.1 109.0 %all-reduce.7.cloned.1.call-start = ((), (), s32[]{:S(2)}) async-start(), calls=%async_computation.7 | async-start | bytes 131072 | tf_op jit(solution)/shard_map/psum | solution.py:43
  206.1 145.4 %all-gather.5.cloned.1.call-start = ((), (), s32[]{:S(2)}) async-start(), calls=%async_computation.12 | async-start | bytes 4718592 | tf_op jit(solution)/shard_map/all_gather | solution.py:46
  256.8 152.9 %all-reduce.9.cloned.1.call-start = ((), (), s32[]{:S(2)}) async-start(), calls=%async_computation.8 | async-start | bytes 131072 | tf_op jit(solution)/shard_map/psum | solution.py:32
  363.9 70.5 %reduce-scatter.9.cloned.1.call-start = ((), (), s32[]{:S(2)}) async-start(), calls=%async_computation.9 | async-start | bytes 655360 | tf_op jit(solution)/shard_map/reduce_scatter | solution.py:37
  409.7 109.6 %reduce-scatter.11.cloned.1.call-start = ((), (), s32[]{:S(2)}) async-start(), calls=%async_computation.10 | async-start | bytes 655360 | tf_op jit(solution)/shard_map/reduce_scatter | solution.py:37
  497.3 109.0 %all-reduce.11.cloned.1.call-start = ((), (), s32[]{:S(2)}) async-start(), calls=%async_computation.11 | async-start | bytes 131072 | tf_op jit(solution)/shard_map/psum | solution.py:43
  536.2 145.4 %all-gather.7.cloned.1.call-start = ((), (), s32[]{:S(2)}) async-start(), calls=%async_computation.13 | async-start | bytes 4718592 | tf_op jit(solution)/shard_map/all_gather | solution.py:46
Sparse Core Ops, SparseCore 0:
  10.9 34.2 all-reduce.4
  71.9 21.7 reduce-scatter.4
  167.2 21.8 reduce-scatter.6
  206.2 69.8 all-reduce.6
  278.6 72.8 all-gather.4
  364.1 30.0 all-reduce.8
  409.8 22.5 reduce-scatter.8
  497.4 21.8 reduce-scatter.10
  536.3 69.8 all-reduce.10
  608.8 72.8 all-gather.6
